TPU v7x, 512 devices: a whole 4x4x16 slice. The times are simulated.
512 devices in a mesh: rep: 8 (over y, core), exp: 64 (over x, z).
Axes of the slice: x: 4, y: 4, z: 16, core: 2. Of those that a mesh axis runs over, the one named last changes fastest.
Arguments:
- payload: bfloat16 [16384, 2048], P(('rep', 'exp')), may hold values from -6 to 6
- block_scales: bfloat16 [16384, 16], P(('rep', 'exp')), may hold values from 0.29882812 to 3
- cotangent: bfloat16 [16384, 2048], P(('rep', 'exp')), may hold values from -12 to 12
- expert_ids: int32 [16384, 8], P(('rep', 'exp')), may hold values from 0 to 63, all different within a row; in each aligned block of 32 rows (0 to 31, 32 to 63, ...) at most 5 rows name the same one
- route_counts: int32 [16384, 8], P(('rep', 'exp')), may hold values from 1 to 15
- gate_up: bfloat16 [64, 2, 2048, 384], P('exp', None, 'rep'), may hold values from -0.125 to 0.125
- down_weight: bfloat16 [64, 384, 2048], P('exp', None, 'rep'), may hold values from -0.3125 to 0.3125
- first_moment: float32 [64, 2, 2048, 384], P('exp', None, 'rep'), may hold values from -12 to 12
- second_moment: float32 [64, 2, 2048, 384], P('exp', None, 'rep'), may hold values from 10 to 300
Outputs:
- d_activation: bfloat16 [16384, 2048], P(('rep', 'exp'))
- new_first: float32 [64, 2, 2048, 384], P('exp', None, 'rep')
- new_second: float32 [64, 2, 2048, 384], P('exp', None, 'rep')
- weight_step: bfloat16 [64, 2, 2048, 384], P('exp', None, 'rep')
Inputs may be any that keep to these rules, and one draw needn't show every extreme that they name: `expert_ids`: in the rows of one device (aligned blocks of 32 tokens) no expert is named more than 5 times, a bound that some block reaches; each token names 8 different experts.
All inputs are finite; a program needn't handle non-finite values.
Results may differ from a plain program's by a relative error of at most 0.02.
Values may be sent and summed in bfloat16 or wider, within the bound.
A program may use at most 64 MiB of HBM per device.

v0:
```python
import jax
import jax.numpy as jnp
from jax import lax
from jax.sharding import PartitionSpec as P


def silu_parts(gate_pre):
    sigmoid_val = jax.nn.sigmoid(gate_pre)
    return (gate_pre * sigmoid_val, sigmoid_val * (1.0 + gate_pre * (1.0 - sigmoid_val)))


def dequantize(values, scales):
    array_shape = values.shape
    blocked = values.astype(jnp.float32).reshape(
        array_shape[:-1] + (scales.shape[-1], array_shape[-1] // scales.shape[-1])
    )
    return (
        (blocked * scales.astype(jnp.float32)[..., None]).reshape(array_shape).astype(jnp.bfloat16)
    )


def rounded_term(input_rows, both_grads, start, count):
    columns = lax.dynamic_slice_in_dim(input_rows, start, count, 1)
    term = jnp.einsum("sd,sf->df", columns, both_grads, preferred_element_type=jnp.float32)
    return lax.optimization_barrier(term.astype(jnp.bfloat16)).astype(jnp.float32)


def on_device(
    payload,
    block_scales,
    cotangent,
    expert_ids,
    route_counts,
    gate_up,
    down_weight,
    first_moment,
    second_moment,
):
    tok_rows, feature_width = payload.shape
    top_count = expert_ids.shape[1]
    experts = lax.axis_size("exp")
    replicas = lax.axis_size("rep")
    capacity = max(2, tok_rows * top_count * 5 // (4 * experts))
    pair_count = tok_rows * top_count
    slot_count = experts * capacity
    flat_ids = expert_ids.reshape(pair_count)
    onehot = (flat_ids[:, None] == jnp.arange(experts, dtype=jnp.int32)[None, :]).astype(jnp.int32)
    slot_rank = jnp.sum((jnp.cumsum(onehot, axis=0) - 1) * onehot, axis=1)
    position = flat_ids * capacity + slot_rank
    slot_table = (
        jnp.full((slot_count,), pair_count, jnp.int32)
        .at[position]
        .set(jnp.arange(pair_count, dtype=jnp.int32))
    )
    filled = (slot_table < pair_count)[:, None]
    pair_index = jnp.minimum(slot_table, pair_count - 1)
    token_index = pair_index // top_count
    count_float = route_counts.astype(jnp.float32)
    route_share = (count_float / jnp.sum(count_float, axis=1, keepdims=True)).reshape(pair_count)
    payload_out = jnp.where(filled, payload[token_index], jnp.zeros((), jnp.bfloat16)).reshape(
        experts, capacity, feature_width
    )
    scales_out = jnp.where(filled, block_scales[token_index], jnp.zeros((), jnp.bfloat16)).reshape(
        experts, capacity, block_scales.shape[1]
    )
    cotan_out = jnp.where(
        filled, route_share[pair_index][:, None] * cotangent[token_index].astype(jnp.float32), 0.0
    )
    cotan_out = cotan_out.astype(jnp.bfloat16).reshape(experts, capacity, feature_width)
    whole_gate_up, whole_down = (
        lax.all_gather(gate_up, "rep", axis=2, tiled=True),
        lax.all_gather(down_weight, "rep", axis=2, tiled=True),
    )
    payload_in, scales_in, cotan_in = (
        lax.all_to_all(payload_out, "exp", split_axis=0, concat_axis=0, tiled=True),
        lax.all_to_all(scales_out, "exp", split_axis=0, concat_axis=0, tiled=True),
        lax.all_to_all(cotan_out, "exp", split_axis=0, concat_axis=0, tiled=True),
    )
    input_rows = dequantize(payload_in, scales_in).reshape(slot_count, feature_width)
    pre_acts = jnp.einsum(
        "sd,tdf->tsf", input_rows, whole_gate_up[0], preferred_element_type=jnp.float32
    )
    cotan_rows = cotan_in.reshape(slot_count, feature_width)
    hidden_grad = jnp.einsum(
        "sd,fd->sf", cotan_rows, whole_down[0], preferred_element_type=jnp.float32
    )
    silu_val, silu_slope = silu_parts(pre_acts[0])
    gate_grad = (hidden_grad * pre_acts[1] * silu_slope).astype(jnp.bfloat16)
    up_grad = (hidden_grad * silu_val).astype(jnp.bfloat16)
    row_grad = (
        jnp.einsum("sf,df->sd", gate_grad, whole_gate_up[0, 0], preferred_element_type=jnp.float32)
        + jnp.einsum("sf,df->sd", up_grad, whole_gate_up[0, 1], preferred_element_type=jnp.float32)
    ).astype(jnp.bfloat16)
    grad_home = lax.all_to_all(
        row_grad.reshape(experts, capacity, feature_width),
        "exp",
        split_axis=0,
        concat_axis=0,
        tiled=True,
    )
    returned = grad_home.reshape(slot_count, feature_width)[position].reshape(
        tok_rows, top_count, feature_width
    )
    d_activation = jnp.sum(returned.astype(jnp.float32), axis=1).astype(jnp.bfloat16)
    hidden_width = gate_grad.shape[1]
    both_grads = jnp.concatenate([gate_grad, up_grad], axis=1)
    block_rows = min(256, feature_width)
    local_square = jnp.zeros((), jnp.float32)
    for block_start in range(0, feature_width, block_rows):
        block_term = rounded_term(input_rows, both_grads, block_start, block_rows)
        local_square = local_square + jnp.sum(block_term * block_term)
    small_sum = lax.psum(local_square, "rep")
    shard_rows = feature_width // replicas
    summed = lax.psum_scatter(
        rounded_term(
            input_rows, both_grads, jnp.int32(0), shard_rows * lax.axis_size("rep")
        ).astype(jnp.bfloat16),
        "rep",
        scatter_dimension=0,
        tiled=True,
    ).astype(jnp.float32)
    grad_shard = summed.reshape(shard_rows, 2, hidden_width).transpose(1, 0, 2)
    shard_square = jnp.sum(grad_shard * grad_shard)
    big_sum = lax.psum(shard_square, "rep")
    entry_count = 2.0 * feature_width * hidden_width
    small_norm = small_sum / (replicas * entry_count)
    big_norm = big_sum / (replicas * replicas * entry_count)
    noise_gain = replicas * big_norm / (small_norm + 1e-06)
    new_first = 0.9 * first_moment + 0.1 * grad_shard[None]
    new_second = 0.95 * second_moment + 0.05 * jnp.square(grad_shard[None])
    weight_step = (noise_gain * new_first / (jnp.sqrt(new_second) + 1e-08)).astype(jnp.bfloat16)
    return (d_activation, new_first, new_second, weight_step)


def solution(mesh):
    in_specs = (
        P(("rep", "exp"), None),
        P(("rep", "exp"), None),
        P(("rep", "exp"), None),
        P(("rep", "exp"), None),
        P(("rep", "exp"), None),
        P("exp", None, "rep", None),
        P("exp", None, "rep"),
        P("exp", None, "rep", None),
        P("exp", None, "rep", None),
    )
    out_specs = (
        P(("rep", "exp"), None),
        P("exp", None, "rep", None),
        P("exp", None, "rep", None),
        P("exp", None, "rep", None),
    )
    return jax.shard_map(
        on_device, mesh=mesh, in_specs=in_specs, out_specs=out_specs, check_vma=False
    )
```

profile of v0, /device:TPU:6, one launch (start us, length us, event | category | flops | bytes accessed | tf_op | source)
XLA Modules:
  0.0 414.0 jit_solution(7159251688583989196)
XLA Ops:
  14.6 19.0 %all-to-all-start.2 = ((bf16[64,5,16]{2,1,0:T(8,128)(2,1)}), bf16[64,5,16]{2,1,0:T(8,128)(2,1)}, u32[]{:S(2)}, u32[]{:S(2)}) async-start(bf16[64,5,16]{2,1,0:T(8,128)(2,1)} %broadcast_select_fusion.1), calls=%async_computation.2 | async-start | bytes 262144 | tf_op jit(solution)/shard_map/all_to_all | solution.py:76
  33.6 2.4 gather_fusion.2
  38.2 10.8 %all-to-all-done.2 = bf16[64,5,16]{2,1,0:T(8,128)(2,1)} async-done(((bf16[64,5,16]{2,1,0:T(8,128)(2,1)}), bf16[64,5,16]{2,1,0:T(8,128)(2,1)}, u32[]{:S(2)}, u32[]{:S(2)}) %all-to-all-start.2) | async-done | bytes 10272 | tf_op jit(solution)/shard_map/all_to_all | solution.py:76
  49.1 6.4 %all-to-all-start.1 = ((bf16[64,5,2048]{2,1,0:T(8,128)(2,1)}), bf16[64,5,2048]{2,1,0:T(8,128)(2,1)S(1)}, u32[]{:S(2)}, u32[]{:S(2)}) async-start(bf16[64,5,2048]{2,1,0:T(8,128)(2,1)} %broadcast_select_fusion), calls=%async_computation.1 | async-start | bytes 4194304 | tf_op jit(solution)/shard_map/all_to_all | solution.py:75
  56.2 3.0 gather_fusion.1
  59.2 3.5 reshape.123
  62.9 2.5 gather_fusion
  65.5 4.0 select_convert_fusion
  69.6 83.6 %all-to-all-done.1 = bf16[64,5,2048]{2,1,0:T(8,128)(2,1)S(1)} async-done(((bf16[64,5,2048]{2,1,0:T(8,128)(2,1)}), bf16[64,5,2048]{2,1,0:T(8,128)(2,1)S(1)}, u32[]{:S(2)}, u32[]{:S(2)}) %all-to-all-start.1) | async-done | bytes 1310752 | tf_op jit(solution)/shard_map/all_to_all | solution.py:75
  154.5 7.8 %all-to-all-start = ((bf16[64,5,2048]{2,1,0:T(8,128)(2,1)}), bf16[64,5,2048]{2,1,0:T(8,128)(2,1)}, u32[]{:S(2)}, u32[]{:S(2)}) async-start(bf16[64,5,2048]{2,1,0:T(8,128)(2,1)} %select_convert_fusion), calls=%async_computation | async-start | bytes 4194304 | tf_op jit(solution)/shard_map/all_to_all | solution.py:77
  166.9 4.0 fusion
  173.0 86.3 %all-to-all-done = bf16[64,5,2048]{2,1,0:T(8,128)(2,1)} async-done(((bf16[64,5,2048]{2,1,0:T(8,128)(2,1)}), bf16[64,5,2048]{2,1,0:T(8,128)(2,1)}, u32[]{:S(2)}, u32[]{:S(2)}) %all-to-all-start) | async-done | bytes 1310752 | tf_op jit(solution)/shard_map/all_to_all | solution.py:77
  259.3 3.6 reshape.118
  262.9 4.0 fusion.7
  266.9 3.0 multiply_convert_fusion
  270.7 3.5 convolution_convert_fusion
  274.2 1.9 copy-done.3
  276.1 2.0 fusion.4
  280.6 8.8 %all-to-all-start.3 = ((bf16[64,5,2048]{2,1,0:T(8,128)(2,1)}), bf16[64,5,2048]{2,1,0:T(8,128)(2,1)S(1)}, u32[]{:S(2)}, u32[]{:S(2)}) async-start(bf16[64,5,2048]{2,1,0:T(8,128)(2,1)} %reshape.120), calls=%async_computation.3 | async-start | bytes 4194304 | tf_op jit(solution)/shard_map/all_to_all | solution.py:94
  289.5 2.3 convolution_convert_fusion.1
  291.8 2.2 convolution_convert_fusion.2
  314.1 72.4 %all-to-all-done.3 = bf16[64,5,2048]{2,1,0:T(8,128)(2,1)S(1)} async-done(((bf16[64,5,2048]{2,1,0:T(8,128)(2,1)}), bf16[64,5,2048]{2,1,0:T(8,128)(2,1)S(1)}, u32[]{:S(2)}, u32[]{:S(2)}) %all-to-all-start.3) | async-done | bytes 1310752 | tf_op jit(solution)/shard_map/all_to_all | solution.py:94
  389.8 1.8 convert_multiply_fusion.1
  391.6 13.0 %all-reduce = (f32[]{:T(128)}, f32[]{:T(128)}) all-reduce(f32[]{:T(128)} %get-tuple-element.12, f32[]{:T(128)S(6)} %add.99), channel_id=1, replica_groups=mesh['rep'=8,'exp'=64] {'rep'}, use_global_device_ids=true, to_apply=%region_8.9 | all-reduce | flops 2 | bytes 16 | tf_op jit(solution)/shard_map/psum | solution.py:124
  (107 shorter events, 41.4 us)
Async XLA Ops:
  7.2 26.5 %copy-start = (bf16[32,2048]{1,0:T(8,128)(2,1)S(1)}, bf16[32,2048]{1,0:T(8,128)(2,1)}, u32[]{:S(2)}) copy-start(bf16[32,2048]{1,0:T(8,128)(2,1)} %param.9) | copy-start | bytes 393220
  14.6 34.4 %all-to-all-start.2 = ((bf16[64,5,16]{2,1,0:T(8,128)(2,1)}), bf16[64,5,16]{2,1,0:T(8,128)(2,1)}, u32[]{:S(2)}, u32[]{:S(2)}) async-start(bf16[64,5,16]{2,1,0:T(8,128)(2,1)} %broadcast_select_fusion.1), calls=%async_computation.2 | async-start | bytes 262144 | tf_op jit(solution)/shard_map/all_to_all | solution.py:76
  38.2 18.0 %copy-start.1 = (bf16[32,2048]{1,0:T(8,128)(2,1)S(1)}, bf16[32,2048]{1,0:T(8,128)(2,1)}, u32[]{:S(2)}) copy-start(bf16[32,2048]{1,0:T(8,128)(2,1)} %param.11) | copy-start | bytes 393220
  49.1 104.1 %all-to-all-start.1 = ((bf16[64,5,2048]{2,1,0:T(8,128)(2,1)}), bf16[64,5,2048]{2,1,0:T(8,128)(2,1)S(1)}, u32[]{:S(2)}, u32[]{:S(2)}) async-start(bf16[64,5,2048]{2,1,0:T(8,128)(2,1)} %broadcast_select_fusion), calls=%async_computation.1 | async-start | bytes 4194304 | tf_op jit(solution)/shard_map/all_to_all | solution.py:75
  55.5 207.5 %all-gather.5.cloned.1.call-start = ((), (), s32[]{:S(2)}) async-start(), calls=%async_computation.6 | async-start | bytes 3538944 | tf_op jit(solution)/shard_map/all_gather | solution.py:71
  59.2 3.5 copy-start.18
  154.5 104.8 %all-to-all-start = ((bf16[64,5,2048]{2,1,0:T(8,128)(2,1)}), bf16[64,5,2048]{2,1,0:T(8,128)(2,1)}, u32[]{:S(2)}, u32[]{:S(2)}) async-start(bf16[64,5,2048]{2,1,0:T(8,128)(2,1)} %select_convert_fusion), calls=%async_computation | async-start | bytes 4194304 | tf_op jit(solution)/shard_map/all_to_all | solution.py:77
  162.4 104.6 %all-gather.3.cloned.1.call-start = ((), (), s32[]{:S(2)}) async-start(), calls=%async_computation.5 | async-start | bytes 1769472 | tf_op jit(solution)/shard_map/all_gather | solution.py:72
  163.1 226.6 %reduce-scatter.2.cloned.1.call-start = ((), (), s32[]{:S(2)}) async-start(), calls=%async_computation.7 | async-start | bytes 3538944 | tf_op jit(solution)/shard_map/reduce_scatter | solution.py:114
  173.0 97.0 %copy-start.5 = (bf16[320,2048]{1,0:T(8,128)(2,1)}, bf16[320,2048]{1,0:T(8,128)(2,1)S(1)}, u32[]{:S(2)}) copy-start(bf16[320,2048]{1,0:T(8,128)(2,1)S(1)} %reshape.119) | copy-start | bytes 3932164
  173.0 90.0 %copy-start.7 = (bf16[320,2048,1]{1,0,2:T(8,128)(2,1)S(1)}, bf16[320,2048,1]{1,0,2:T(8,128)(2,1)}, u32[]{:S(2)}) copy-start(bf16[320,2048,1]{1,0,2:T(8,128)(2,1)} %reshape.176) | copy-start | bytes 3932164
  274.2 1.9 copy-start.3
  276.1 2.0 copy-start.4
  276.1 2.0 copy-start.16
  280.6 8.8 %copy-start.20 = (s32[256,1]{0,1:T(1,128)S(1)}, s32[256,1]{0,1:T(1,128)}, u32[]{:S(2)}) copy-start(s32[256,1]{0,1:T(1,128)} %copy-done.19) | copy-start | bytes 3076
  280.6 8.9 %copy-start.6 = (bf16[320,2048]{1,0:T(8,128)(2,1)S(1)}, bf16[320,2048]{1,0:T(8,128)(2,1)}, u32[]{:S(2)}) copy-start(bf16[320,2048]{1,0:T(8,128)(2,1)} %copy-done.5) | copy-start | bytes 3932164
  280.6 105.8 %all-to-all-start.3 = ((bf16[64,5,2048]{2,1,0:T(8,128)(2,1)}), bf16[64,5,2048]{2,1,0:T(8,128)(2,1)S(1)}, u32[]{:S(2)}, u32[]{:S(2)}) async-start(bf16[64,5,2048]{2,1,0:T(8,128)(2,1)} %reshape.120), calls=%async_computation.3 | async-start | bytes 4194304 | tf_op jit(solution)/shard_map/all_to_all | solution.py:94
  289.5 4.6 %copy-start.11 = (bf16[320,384]{1,0:T(8,128)(2,1)S(1)}, bf16[320,384]{1,0:T(8,128)(2,1)}, u32[]{:S(2)}) copy-start(bf16[320,384]{1,0:T(8,128)(2,1)} %copy-done.10) | copy-start | bytes 737284
  289.5 4.6 %copy-start.17 = (bf16[320,384]{1,0:T(8,128)(2,1)S(1)}, bf16[320,384]{1,0:T(8,128)(2,1)}, u32[]{:S(2)}) copy-start(bf16[320,384]{1,0:T(8,128)(2,1)} %copy-done.15) | copy-start | bytes 737284
  299.5 10.2 %copy-start.14 = (bf16[256,768]{1,0:T(8,128)(2,1)S(1)}, bf16[256,768]{1,0:T(8,128)(2,1)}, u32[]{:S(2)}) copy-start(bf16[256,768]{1,0:T(8,128)(2,1)} %convolution_convert_fusion.3) | copy-start | bytes 1179652
  299.5 11.7 %copy-start.13 = (bf16[256,768]{1,0:T(8,128)(2,1)S(1)}, bf16[256,768]{1,0:T(8,128)(2,1)}, u32[]{:S(2)}) copy-start(bf16[256,768]{1,0:T(8,128)(2,1)} %convolution_convert_fusion.2) | copy-start | bytes 1179652
  299.5 13.1 %copy-start.12 = (bf16[256,768]{1,0:T(8,128)(2,1)S(1)}, bf16[256,768]{1,0:T(8,128)(2,1)}, u32[]{:S(2)}) copy-start(bf16[256,768]{1,0:T(8,128)(2,1)} %convolution_convert_fusion.1) | copy-start | bytes 1179652
  388.4 17.6 %copy-start.8 = (f32[1,2,256,384]{3,2,1,0:T(8,128)S(1)}, f32[1,2,256,384]{3,2,1,0:T(8,128)}, u32[]{:S(2)}) copy-start(f32[1,2,256,384]{3,2,1,0:T(8,128)} %param.17) | copy-start | bytes 2359300
  388.4 17.6 %copy-start.9 = (f32[1,2,256,384]{3,2,1,0:T(8,128)S(1)}, f32[1,2,256,384]{3,2,1,0:T(8,128)}, u32[]{:S(2)}) copy-start(f32[1,2,256,384]{3,2,1,0:T(8,128)} %param.16) | copy-start | bytes 2359300
  (4 other events, 4.3 us)
Sparse Core Ops, SparseCore 0:
  58.4 36.1 all-gather.4
  165.3 33.3 all-gather.2
  274.4 38.3 reduce-scatter.1
where the time goes:
time: 417 us; the launch traced here: 414 us
  waiting for transfers between devices  255 us (61%)
  starting transfers between devices  42.3 us (10%)
  local copies, waits for them, and re-layouts  34.3 us (8%)
  other arithmetic  25.9 us (6%)
  matrix products  23.3 us (6%)
  between operations  20.6 us (5%)
  blocking collectives  13 us (3%)
    all_to_all x1, waiting for transfers between devices, on_device(): lax.all_to_all(cotan_out, 'exp', split_axis=0, concat_axis=0, tiled=True)  86.3 us
    all_to_all x1, waiting for transfers between devices, on_device(): lax.all_to_all(payload_out, 'exp', split_axis=0, concat_axis=0, tiled=True)  83.6 us
    all_to_all x1, waiting for transfers between devices, on_device(): lax.all_to_all(row_grad.reshape(experts, capacity, feature_width), 'exp',...  72.4 us
    all_to_all x1, starting transfers between devices, on_device(): lax.all_to_all(scales_out, 'exp', split_axis=0, concat_axis=0, tiled=True)  19 us
    dot_general x9, matrix products, rounded_term(): jnp.einsum('sd,sf->df', columns, both_grads, preferred_element_type=jnp.f...  13.5 us
    psum x1, blocking collectives, on_device(): big_sum = lax.psum(shard_square, 'rep')  13 us
    all_to_all x1, waiting for transfers between devices, on_device(): lax.all_to_all(scales_out, 'exp', split_axis=0, concat_axis=0, tiled=True)  10.8 us
    reduce_sum x8, other arithmetic, on_device(): local_square = local_square + jnp.sum(block_term * block_term)  9.41 us
  transfers between devices with their start and end apart: 7, of which 4 were waited for; matrix products, arithmetic and copies ran while one was open for 15% of the time, Pallas kernels for 0%

commit v1 on v0

v1 whole, which is shorter than its diff:
```python
import jax
import jax.numpy as jnp
import numpy as np
from jax import lax
from jax.sharding import PartitionSpec as P

X_SIZE = 4
Z_SIZE = 16
CAPACITY = 5
Z_GROUPS = [[x * Z_SIZE + z for z in range(Z_SIZE)] for x in range(X_SIZE)]
X_GROUPS = [[x * Z_SIZE + z for x in range(X_SIZE)] for z in range(Z_SIZE)]


def silu_parts(gate_pre):
    sigmoid_val = jax.nn.sigmoid(gate_pre)
    return (gate_pre * sigmoid_val, sigmoid_val * (1.0 + gate_pre * (1.0 - sigmoid_val)))


def dequantize(values, scales):
    array_shape = values.shape
    blocked = values.astype(jnp.float32).reshape(
        array_shape[:-1] + (scales.shape[-1], array_shape[-1] // scales.shape[-1])
    )
    return (
        (blocked * scales.astype(jnp.float32)[..., None]).reshape(array_shape).astype(jnp.bfloat16)
    )


def route_tables(ids, counts, z_pos, tok_rows):
    count_float = counts.astype(jnp.float32)
    share = count_float / jnp.sum(count_float, axis=1, keepdims=True)
    experts = jnp.arange(X_SIZE, dtype=jnp.int32) * Z_SIZE + z_pos
    hit = ids[None] == experts[:, None, None]
    match = jnp.any(hit, axis=2)
    weight = jnp.sum(jnp.where(hit, share[None], 0.0), axis=2)
    ones = match.astype(jnp.bfloat16).reshape(X_SIZE * Z_SIZE, tok_rows)
    before = jnp.asarray(np.triu(np.ones((tok_rows, tok_rows)), 1), jnp.bfloat16)
    rank = jnp.dot(ones, before, preferred_element_type=jnp.float32).astype(jnp.int32)
    base = jnp.arange(Z_SIZE, dtype=jnp.int32)[None, :, None] * CAPACITY
    slot = (base + rank.reshape(X_SIZE, Z_SIZE, tok_rows)).reshape(X_SIZE, Z_SIZE * tok_rows)
    slot = jnp.where(match, slot, -1)
    lanes = jnp.arange(Z_SIZE * CAPACITY, dtype=jnp.int32)
    pick = slot[:, None, :] == lanes[None, :, None]
    slot_share = jnp.sum(jnp.where(pick, weight[:, None, :], 0.0), axis=2)
    pick = pick.reshape(X_SIZE * Z_SIZE * CAPACITY, Z_SIZE * tok_rows).astype(jnp.bfloat16)
    return pick, slot_share.reshape(X_SIZE * Z_SIZE * CAPACITY)


def on_device(
    payload,
    block_scales,
    cotangent,
    expert_ids,
    route_counts,
    gate_up,
    down_weight,
    first_moment,
    second_moment,
):
    tok_rows, width = payload.shape
    replicas = lax.axis_size("rep")
    z_pos = lax.axis_index("exp") % Z_SIZE
    side = Z_SIZE * CAPACITY
    slot_count = X_SIZE * side

    activation = dequantize(payload, block_scales)
    routing = jnp.concatenate([expert_ids, route_counts], axis=1).astype(jnp.bfloat16)
    routing = jnp.pad(routing, ((0, 0), (0, 112)))
    act_all = lax.all_gather(
        jnp.concatenate([activation, routing], axis=1),
        "exp",
        axis=0,
        tiled=True,
        axis_index_groups=Z_GROUPS,
    )
    cot_all = lax.all_gather(cotangent, "exp", axis=0, tiled=True, axis_index_groups=Z_GROUPS)
    whole_gate_up = lax.all_gather(gate_up, "rep", axis=2, tiled=True)
    whole_down = lax.all_gather(down_weight, "rep", axis=2, tiled=True)

    top = expert_ids.shape[1]
    ids = act_all[:, width : width + top].astype(jnp.int32)
    counts = act_all[:, width + top : width + 2 * top].astype(jnp.int32)
    pick, slot_share = route_tables(ids, counts, z_pos, tok_rows)

    def to_experts(rows):
        return lax.all_to_all(
            rows.reshape(X_SIZE, side, width),
            "exp",
            split_axis=0,
            concat_axis=0,
            tiled=True,
            axis_index_groups=X_GROUPS,
        )

    act_rows = jnp.dot(pick, act_all[:, :width], preferred_element_type=jnp.float32)
    input_rows = to_experts(act_rows.astype(jnp.bfloat16)).reshape(slot_count, width)
    cot_rows = jnp.dot(pick, cot_all, preferred_element_type=jnp.float32)
    cot_rows = (slot_share[:, None] * cot_rows).astype(jnp.bfloat16)
    cotan_rows = to_experts(cot_rows).reshape(slot_count, width)

    pre_acts = jnp.einsum(
        "sd,tdf->tsf", input_rows, whole_gate_up[0], preferred_element_type=jnp.float32
    )
    hidden_grad = jnp.einsum(
        "sd,fd->sf", cotan_rows, whole_down[0], preferred_element_type=jnp.float32
    )
    silu_val, silu_slope = silu_parts(pre_acts[0])
    gate_grad = (hidden_grad * pre_acts[1] * silu_slope).astype(jnp.bfloat16)
    up_grad = (hidden_grad * silu_val).astype(jnp.bfloat16)
    row_grad = (
        jnp.einsum("sf,df->sd", gate_grad, whole_gate_up[0, 0], preferred_element_type=jnp.float32)
        + jnp.einsum("sf,df->sd", up_grad, whole_gate_up[0, 1], preferred_element_type=jnp.float32)
    ).astype(jnp.bfloat16)
    home = to_experts(row_grad).reshape(slot_count, width)
    partial = jnp.einsum("st,sd->td", pick, home, preferred_element_type=jnp.float32)
    d_activation = lax.psum_scatter(
        partial.astype(jnp.bfloat16),
        "exp",
        scatter_dimension=0,
        tiled=True,
        axis_index_groups=Z_GROUPS,
    )

    hidden_width = gate_grad.shape[1]
    both_grads = jnp.concatenate([gate_grad, up_grad], axis=1)
    term = jnp.einsum("sd,sf->df", input_rows, both_grads, preferred_element_type=jnp.float32)
    term = lax.optimization_barrier(term.astype(jnp.bfloat16))
    local_square = jnp.sum(jnp.square(term.astype(jnp.float32)))
    summed = lax.psum_scatter(term, "rep", scatter_dimension=0, tiled=True).astype(jnp.float32)
    shard_rows = width // replicas
    grad_shard = summed.reshape(shard_rows, 2, hidden_width).transpose(1, 0, 2)
    small_sum, big_sum = lax.psum((local_square, jnp.sum(jnp.square(grad_shard))), "rep")
    entry_count = 2.0 * width * hidden_width
    small_norm = small_sum / (replicas * entry_count)
    big_norm = big_sum / (replicas * replicas * entry_count)
    noise_gain = replicas * big_norm / (small_norm + 1e-06)
    new_first = 0.9 * first_moment + 0.1 * grad_shard[None]
    new_second = 0.95 * second_moment + 0.05 * jnp.square(grad_shard[None])
    weight_step = (noise_gain * new_first / (jnp.sqrt(new_second) + 1e-08)).astype(jnp.bfloat16)
    return (d_activation, new_first, new_second, weight_step)


def solution(mesh):
    tokens = P(("rep", "exp"), None)
    shards = P("exp", None, "rep", None)
    return jax.shard_map(
        on_device,
        mesh=mesh,
        in_specs=(tokens,) * 5 + (shards, P("exp", None, "rep"), shards, shards),
        out_specs=(tokens, shards, shards, shards),
        check_vma=False,
    )
```

time: 417 us -> 366 us (0.88)
  starting transfers between devices: 42.3 us -> 9.77 us
  local copies, waits for them, and re-layouts: 34.3 us -> 6.8 us
  blocking collectives: 13 us -> 34.4 us
  other arithmetic: 25.9 us -> 7.83 us
  waiting for transfers between devices: 255 us -> 269 us
  between operations: 20.6 us -> 15.6 us
    all_to_all x4 -> x2, waiting for transfers between devices: 253 us -> 0.01 us  [to_experts(): lax.all_to_all(rows.reshape(X_SIZE, side, width), 'exp', split_axis=0, co...]
    all_gather x2 -> x4, waiting for transfers between devices: 0.01 us -> 193 us  [the longest x1 75.3 us: on_device(): lax.all_gather(jnp.concatenate([activation, routing], axis=1), 'exp', axi...]
    reduce_scatter x1 -> x2, waiting for transfers between devices: 0.01 us -> 73.6 us  [the longest x1 58.1 us: on_device(): lax.psum_scatter(partial.astype(jnp.bfloat16), 'exp', scatter_dimension=0...]
    all_to_all x4 -> x2, starting transfers between devices: 42 us -> 9.57 us  [to_experts(): lax.all_to_all(rows.reshape(X_SIZE, side, width), 'exp', split_axis=0, co...]
    all_to_all x0 -> x1, blocking collectives: none -> 20.8 us  [to_experts(): lax.all_to_all(rows.reshape(X_SIZE, side, width), 'exp', split_axis=0, co...]
    gather x7 -> x0, local copies, waits for them, and re-layouts: 11.3 us -> none  [the longest x1 3.02 us: on_device(): cotangent[token_index].astype(jnp.float32)]
    reduce_sum x11 -> x4, other arithmetic: 10.9 us -> 2.5 us  [the longest x1 2.22 us: on_device(): local_square = jnp.sum(jnp.square(term.astype(jnp.float32)))]
    reshape x6 -> x2, local copies, waits for them, and re-layouts: 7.91 us -> 0.18 us  [the longest x1 0.09 us: route_tables(): rank.reshape(X_SIZE, Z_SIZE, tok_rows)]
  transfers between devices with their start and end apart: 7 -> 8, of which waited for: 4 -> 6; matrix products, arithmetic and copies ran while one was open for 15% -> 6% of each run, Pallas kernels for 0% -> 0%
where the time goes in v1:
time: 366 us; the launch traced here: 365 us
  waiting for transfers between devices  269 us (73%)
  blocking collectives  34.4 us (9%)
  matrix products  21.7 us (6%)
  between operations  15.6 us (4%)
  starting transfers between devices  9.77 us (3%)
  other arithmetic  7.83 us (2%)
  local copies, waits for them, and re-layouts  6.8 us (2%)
    all_gather x1, waiting for transfers between devices, on_device(): lax.all_gather(jnp.concatenate([activation, routing], axis=1), 'exp', axi...  75.3 us
    all_gather x1, waiting for transfers between devices, on_device(): lax.all_gather(cotangent, 'exp', axis=0, tiled=True, axis_index_groups=Z_...  61.3 us
    reduce_scatter x1, waiting for transfers between devices, on_device(): lax.psum_scatter(partial.astype(jnp.bfloat16), 'exp', scatter_dimension=0...  58.1 us
    all_gather x1, waiting for transfers between devices, on_device(): whole_down = lax.all_gather(down_weight, 'rep', axis=2, tiled=True)  30.6 us
    all_gather x1, waiting for transfers between devices, on_device(): whole_gate_up = lax.all_gather(gate_up, 'rep', axis=2, tiled=True)  26.2 us
    all_to_all x1, blocking collectives, to_experts(): lax.all_to_all(rows.reshape(X_SIZE, side, width), 'exp', split_axis=0, co...  20.8 us
    reduce_scatter x1, waiting for transfers between devices, on_device(): lax.psum_scatter(term, 'rep', scatter_dimension=0, tiled=True)  15.5 us
    psum x1, blocking collectives, on_device(): lax.psum((local_square, jnp.sum(jnp.square(grad_shard))), 'rep')  13.5 us
  transfers between devices with their start and end apart: 8, of which 6 were waited for; matrix products, arithmetic and copies ran while one was open for 6% of the time, Pallas kernels for 0%

profile of v1, /device:TPU:6, one launch (start us, length us, event | category | flops | bytes accessed | tf_op | source)
XLA Modules:
  0.0 364.9 jit_solution(17802854460447803655)
XLA Ops:
  9.7 1.0 fusion.22
  13.8 75.3 %all-gather.5.cloned.1.call-done = bf16[512,2176]{1,0:T(8,128)(2,1)} async-done(((bf16[32,2176]{1,0:T(8,128)(2,1)}), bf16[512,2176]{1,0:T(8,128)(2,1)}) %all-gather.5.cloned.1.call-update) | async-done | bytes 2228240 | tf_op jit(solution)/shard_map/all_gather | solution.py:69
  89.0 1.1 fusion.30
  91.0 3.5 convolution_convert_fusion.1
  94.5 4.8 %all-to-all-start.1 = ((bf16[4,80,2048]{2,1,0:T(8,128)(2,1)}), bf16[4,80,2048]{2,1,0:T(8,128)(2,1)S(1)}, u32[]{:S(2)}, u32[]{:S(2)}) async-start(bf16[4,80,2048]{2,1,0:T(8,128)(2,1)} %bitcast.4), calls=%async_computation.1 | async-start | bytes 2621440 | tf_op jit(solution)/shard_map/all_to_all | solution.py:86
  99.7 61.3 %all-gather.7.cloned.1.call-done = bf16[512,2048]{1,0:T(8,128)(2,1)} async-done(((bf16[32,2048]{1,0:T(8,128)(2,1)}), bf16[512,2048]{1,0:T(8,128)(2,1)}) %all-gather.7.cloned.1.call-update) | async-done | bytes 2097168 | tf_op jit(solution)/shard_map/all_gather | solution.py:76
  161.0 3.5 fusion.3
  164.5 4.8 %all-to-all-start = ((bf16[4,80,2048]{2,1,0:T(8,128)(2,1)}), bf16[4,80,2048]{2,1,0:T(8,128)(2,1)S(1)}, u32[]{:S(2)}, u32[]{:S(2)}) async-start(bf16[4,80,2048]{2,1,0:T(8,128)(2,1)} %bitcast.1), calls=%async_computation | async-start | bytes 2621440 | tf_op jit(solution)/shard_map/all_to_all | solution.py:86
  169.3 26.2 %all-gather.11.cloned.1.call-done = bf16[1,2,2048,384]{3,2,1,0:T(8,128)(2,1)} async-done(((bf16[1,2,256,384]{3,2,1,0:T(8,128)(2,1)}), bf16[1,2,2048,384]{3,2,1,0:T(8,128)(2,1)}) %all-gather.11.cloned.1.call-update) | async-done | bytes 3145744 | tf_op jit(solution)/shard_map/all_gather | solution.py:77
  195.5 4.0 %fusion.8 = f32[2,320,384]{2,1,0:T(8,128)} fusion(bf16[320,2048,1]{1,0,2:T(8,128)(2,1)S(1)} %bitcast.88, bf16[1,2,2048,384]{3,2,1,0:T(8,128)(2,1)} %all-gather.11.cloned.1.call-done), kind=kOutput, calls=%fused_computation.16 | convolution fusion | flops 1006632960 | bytes 5439488 | tf_op jit(solution)/shard_map/sd,tdf->tsf/dot_general | solution.py:101
  199.5 30.6 %all-gather.9.cloned.1.call-done = bf16[1,384,2048]{2,1,0:T(8,128)(2,1)} async-done(((bf16[1,384,256]{2,1,0:T(8,128)(2,1)}), bf16[1,384,2048]{2,1,0:T(8,128)(2,1)}) %all-gather.9.cloned.1.call-update) | async-done | bytes 1572880 | tf_op jit(solution)/shard_map/all_gather | solution.py:78
  230.1 2.6 multiply_convert_fusion
  233.4 3.5 convolution_convert_fusion
  237.0 1.8 copy-done.1
  238.8 0.9 fusion.5
  239.7 0.9 fusion.2
  240.6 20.8 %all_to_all.15 = bf16[4,80,2048]{2,1,0:T(8,128)(2,1)S(1)} all-to-all(bf16[4,80,2048]{2,1,0:T(8,128)(2,1)S(1)} %bitcast.85), channel_id=1, replica_groups={{0,16,32,48},{1,17,33,49},{2,18,34,50},{3,19,35,51},{4,20,36,52},{5,21,..., dimensions={0} | all-to-all | bytes 2621440 | tf_op jit(solution)/shard_map/all_to_all | solution.py:86
  261.5 2.7 bitcast_convert_fusion
  264.1 2.2 multiply_reduce_fusion
  266.4 15.5 %reduce-scatter.5.cloned.1.call-done = bf16[256,768]{1,0:T(8,128)(2,1)} async-done(((bf16[2048,768]{1,0:T(8,128)(2,1)}), bf16[256,768]{1,0:T(8,128)(2,1)}) %reduce-scatter.5.cloned.1.call-update) | async-done | bytes 393232 | tf_op jit(solution)/shard_map/reduce_scatter | solution.py:129
  281.8 1.8 convert_multiply_fusion.1
  283.6 13.5 %all-reduce.1 = (f32[]{:T(128)}, f32[]{:T(128)}) all-reduce(f32[]{:T(128)} %get-tuple-element.14, f32[]{:T(128)} %multiply_reduce_fusion), channel_id=1, replica_groups=mesh['rep'=8,'exp'=64] {'rep'}, use_global_device_ids=true, to_apply=%region_7.8 | all-reduce | flops 2 | bytes 16 | tf_op jit(solution)/shard_map/psum | solution.py:132
  298.5 1.4 divide_convert_fusion
  300.0 58.1 %reduce-scatter.3.cloned.1.call-done = bf16[32,2048]{1,0:T(8,128)(2,1)} async-done(((bf16[512,2048]{1,0:T(8,128)(2,1)}), bf16[32,2048]{1,0:T(8,128)(2,1)}) %reduce-scatter.3.cloned.1.call-update) | async-done | bytes 131088 | tf_op jit(solution)/shard_map/reduce_scatter | solution.py:116
  (56 shorter events, 7.6 us)
Async XLA Ops:
  7.2 83.3 %copy-start.6 = (bf16[32,32]{1,0:T(8,128)(2,1)S(1)}, bf16[32,32]{1,0:T(8,128)(2,1)}, u32[]{:S(2)}) copy-start(bf16[32,32]{1,0:T(8,128)(2,1)} %constant.52.clone) | copy-start | bytes 6148
  7.2 81.9 %all-gather.5.cloned.1.call-start = ((), (), s32[]{:S(2)}) async-start(), calls=%async_computation.5 | async-start | bytes 2367488 | tf_op jit(solution)/shard_map/all_gather | solution.py:69
  11.4 149.6 %all-gather.7.cloned.1.call-start = ((), (), s32[]{:S(2)}) async-start(), calls=%async_computation.6 | async-start | bytes 2228224 | tf_op jit(solution)/shard_map/all_gather | solution.py:76
  12.2 183.3 %all-gather.11.cloned.1.call-start = ((), (), s32[]{:S(2)}) async-start(), calls=%async_computation.8 | async-start | bytes 3538944 | tf_op jit(solution)/shard_map/all_gather | solution.py:77
  12.9 217.2 %all-gather.9.cloned.1.call-start = ((), (), s32[]{:S(2)}) async-start(), calls=%async_computation.7 | async-start | bytes 1769472 | tf_op jit(solution)/shard_map/all_gather | solution.py:78
  94.5 70.1 %all-to-all-start.1 = ((bf16[4,80,2048]{2,1,0:T(8,128)(2,1)}), bf16[4,80,2048]{2,1,0:T(8,128)(2,1)S(1)}, u32[]{:S(2)}, u32[]{:S(2)}) async-start(bf16[4,80,2048]{2,1,0:T(8,128)(2,1)} %bitcast.4), calls=%async_computation.1 | async-start | bytes 2621440 | tf_op jit(solution)/shard_map/all_to_all | solution.py:86
  164.5 65.6 %all-to-all-start = ((bf16[4,80,2048]{2,1,0:T(8,128)(2,1)}), bf16[4,80,2048]{2,1,0:T(8,128)(2,1)S(1)}, u32[]{:S(2)}, u32[]{:S(2)}) async-start(bf16[4,80,2048]{2,1,0:T(8,128)(2,1)} %bitcast.1), calls=%async_computation | async-start | bytes 2621440 | tf_op jit(solution)/shard_map/all_to_all | solution.py:86
  169.3 112.5 %reduce-scatter.5.cloned.1.call-start = ((), (), s32[]{:S(2)}) async-start(), calls=%async_computation.10 | async-start | bytes 3538944 | tf_op jit(solution)/shard_map/reduce_scatter | solution.py:129
  232.7 0.7 copy-start.4
  236.9 1.9 copy-start.1
  236.9 121.2 %reduce-scatter.3.cloned.1.call-start = ((), (), s32[]{:S(2)}) async-start(), calls=%async_computation.9 | async-start | bytes 2228224 | tf_op jit(solution)/shard_map/reduce_scatter | solution.py:116
  238.8 0.9 copy-start.5
  261.5 2.7 copy-start
  266.4 32.1 %copy-start.2 = (f32[1,2,256,384]{3,2,1,0:T(8,128)S(1)}, f32[1,2,256,384]{3,2,1,0:T(8,128)}, u32[]{:S(2)}) copy-start(f32[1,2,256,384]{3,2,1,0:T(8,128)} %param.18) | copy-start | bytes 2359300
  266.4 32.1 %copy-start.3 = (f32[1,2,256,384]{3,2,1,0:T(8,128)S(1)}, f32[1,2,256,384]{3,2,1,0:T(8,128)}, u32[]{:S(2)}) copy-start(f32[1,2,256,384]{3,2,1,0:T(8,128)} %param.17) | copy-start | bytes 2359300
Sparse Core Ops, SparseCore 0:
  11.6 77.4 all-gather.4
  91.1 69.8 all-gather.6
  163.2 32.2 all-gather.10
  197.4 32.5 all-gather.8
  237.0 44.7 reduce-scatter.4
  285.1 72.9 reduce-scatter.2
